TPU v7x, 256 devices: a whole 4x4x8 slice. The times are simulated.
256 devices in a mesh: leaf: 64 (over z, y, core), rhs: 4 (over x).
Axes of the slice: x: 4, y: 4, z: 8, core: 2. Of those that a mesh axis runs over, the one named last changes fastest.
Arguments:
- densities: bfloat16 [64, 262144], P('rhs', 'leaf'), may hold values from -6 to 6
- bases: float32 [32, 262144], P(None, 'leaf'), may hold values from -0.5 to 0.5
- near_blocks: bfloat16 [2048, 8, 128, 128], P('leaf', 'rhs'), may hold values from -0.1875 to 0.1875
- near_src: int32 [2048, 8], P('leaf', 'rhs'), may hold values from 0 to 55, as said below
- send_leaf: int32 [64, 6, 4], replicated, may hold values from -1 to 31, as said below
- far_src: int32 [2048, 8], P('leaf'), may hold values from 0 to 31
- leaf_coupling: float32 [2048, 8, 32, 32], P('leaf'), may hold values from -0.375 to 0.375
- local_transfer: float32 [64, 64, 32, 32], P('leaf'), may hold values from -0.75 to 0.75
- upper_transfer: float32 [128, 32, 32], replicated, may hold values from -0.75 to 0.75
- up_coupling: float32 [128, 3, 32, 32], replicated, may hold values from -8 to 8
Outputs:
- product: float32 [64, 262144], P('rhs', 'leaf')
Inputs may be any that keep to these rules, and one draw needn't show every extreme that they name: `send_leaf`: entry [e, j, c] is a leaf of device e (local index) whose panel e sends to its face neighbour e + o_j, or -1. Only existing face neighbours receive; the leaves of [e, j] are distinct and come before the -1 entries; every device sends exactly 4 leaves to at least one neighbour, among them its leaf 32 - 1, and exactly 4 to its neighbour at offset -s*s where that exists. `near_src`: A slot of the owner's panel buffer: below 32 a leaf of the same device, else slot 32 + j * 4 + c. It never names an empty slot, and every filled slot is named by some block of the device.
All inputs are finite; a program needn't handle non-finite values.
Results may differ from a plain program's by a relative error of at most 0.0003.
Values may be sent and summed in bfloat16 or wider, within the bound.
A program may use at most 128 MiB of HBM per device.

v0:
```python
import jax
import jax.numpy as jnp
from jax import lax
from jax.sharding import PartitionSpec as P

TOP_PREC = lax.Precision.HIGHEST
FACE_SIGNS = ((1, 0), (-1, 0), (1, 1), (-1, 1), (1, 2), (-1, 2))


def shifted(value, axis, steps):
    count = lax.axis_size(axis)
    first, last = (max(0, -steps), min(count, count - steps))
    return lax.ppermute(value, axis, [(source, source + steps) for source in range(first, last)])


def from_everyone(x, axis):
    copies = jnp.broadcast_to(x, (lax.axis_size(axis), *x.shape))
    return lax.all_to_all(copies, axis, split_axis=0, concat_axis=0, tiled=True)


def laid_out(parts, dim):
    parts = jnp.moveaxis(parts, 0, dim)
    shape = parts.shape
    return parts.reshape(*shape[:dim], shape[dim] * shape[dim + 1], *shape[dim + 2 :])


def gather_directly(x, axis, dim):
    parts = from_everyone(x, axis)
    return laid_out(parts, dim)


def cube_side(device_count):
    return max((edge_len for edge_len in range(1, 65) if edge_len**3 <= device_count))


def face_offsets(device_count):
    side_len = cube_side(device_count)
    return [face_sign * side_len**axis_pos for face_sign, axis_pos in FACE_SIGNS]


def lift_pairs(child_coef, child_maps):
    lifted = jnp.einsum("...nrs,...nqr->...nqs", child_maps, child_coef, precision=TOP_PREC)
    return lifted[..., 0::2, :, :] + lifted[..., 1::2, :, :]


def apply_maps(node_maps, coef_rows):
    return jnp.einsum("...nrs,...nqs->...nqr", node_maps, coef_rows, precision=TOP_PREC)


def couple_level(coef_level, maps_level):
    level_width = coef_level.shape[0]
    even_node = jnp.arange(level_width) % 2 == 0
    padded = jnp.pad(coef_level, ((3, 3), (0, 0), (0, 0)))
    minus_two = padded[1 : level_width + 1]
    plus_two = padded[5 : level_width + 5]
    third_node = jnp.where(
        even_node[:, None, None], padded[6 : level_width + 6], padded[0:level_width]
    )
    first_terms = apply_maps(maps_level[:, 0], minus_two) + apply_maps(maps_level[:, 1], plus_two)
    return first_terms + apply_maps(maps_level[:, 2], third_node)


def upper_tree(roots, upper_transfer, up_coupling):
    node_total = roots.shape[0]
    coef_levels = {node_total: roots}
    level_width = node_total
    while level_width > 4:
        coef_levels[level_width // 2] = lift_pairs(
            coef_levels[level_width], upper_transfer[level_width : 2 * level_width]
        )
        level_width = level_width // 2
    level_field = couple_level(coef_levels[4], up_coupling[4:8])
    level_width = 4
    while level_width < node_total:
        level_width = level_width * 2
        coupled = couple_level(coef_levels[level_width], up_coupling[level_width : 2 * level_width])
        level_field = coupled + apply_maps(
            upper_transfer[level_width : 2 * level_width], jnp.repeat(level_field, 2, axis=0)
        )
    return level_field


def local(
    densities,
    bases,
    near_blocks,
    near_src,
    send_leaf,
    far_src,
    leaf_coupling,
    local_transfer,
    upper_transfer,
    up_coupling,
):
    leaf_devices = lax.axis_size("leaf")
    device_rank = lax.axis_index("leaf")
    columns, points = densities.shape
    leaf_count = near_blocks.shape[0]
    leaf_width = near_blocks.shape[2]
    rank_width = bases.shape[0]
    panels = densities.reshape(columns, leaf_count, leaf_width)
    offsets = face_offsets(leaf_devices)
    arrived = []
    for direction in range(6):
        neighbour_panels = shifted(panels, "leaf", offsets[direction])
        sender = device_rank - offsets[direction]
        inside = (sender >= 0) & (sender < leaf_devices)
        clipped = jnp.clip(sender, 0, leaf_devices - 1)
        sent_leaf = lax.dynamic_index_in_dim(send_leaf, clipped, 0, keepdims=False)[direction]
        chosen = jnp.take(neighbour_panels, jnp.maximum(sent_leaf, 0), axis=1)
        keep_slot = inside & (sent_leaf >= 0)
        arrived.append(jnp.where(keep_slot[None, :, None], chosen, jnp.zeros_like(chosen)))
    buffer = jnp.concatenate([panels] + arrived, axis=1)
    piece_blocks = lax.all_gather(near_blocks, "rhs", axis=1, tiled=True)
    piece_sources = lax.all_gather(near_src, "rhs", axis=1, tiled=True)
    picked = jnp.take(buffer, piece_sources, axis=1)
    near_field = jnp.einsum(
        "tkij,qtkj->qti", piece_blocks, picked, preferred_element_type=jnp.float32
    )
    near_field = near_field.reshape(columns, points)
    basis_view = bases.reshape(rank_width, leaf_count, leaf_width)
    leaf_coef = jnp.einsum(
        "rti,qti->tqr", basis_view, panels.astype(jnp.float32), precision=TOP_PREC
    )
    subtree_maps = local_transfer[0]
    coef_levels = {leaf_count: leaf_coef}
    level_width = leaf_count
    while level_width > 1:
        coef_levels[level_width // 2] = lift_pairs(
            coef_levels[level_width], subtree_maps[level_width : 2 * level_width]
        )
        level_width = level_width // 2
    root_coef = coef_levels[1][0]
    roots = gather_directly(root_coef[None], "leaf", 0)
    root_all = upper_tree(roots, upper_transfer, up_coupling)
    root_field = lax.dynamic_index_in_dim(root_all, device_rank, 0, keepdims=False)
    picked_coef = jnp.take(leaf_coef, far_src, axis=0)
    leaf_local = jnp.einsum("tjrs,tjqs->tqr", leaf_coupling, picked_coef, precision=TOP_PREC)
    level_field = root_field[None]
    level_width = 1
    while level_width < leaf_count:
        level_width = level_width * 2
        level_field = apply_maps(
            subtree_maps[level_width : 2 * level_width], jnp.repeat(level_field, 2, axis=0)
        )
    leaf_field = level_field + leaf_local
    far_part = jnp.einsum("rti,tqr->qti", basis_view, leaf_field, precision=TOP_PREC).reshape(
        columns, points
    )
    return near_field + far_part


def solution(mesh):
    in_specs = (
        P("rhs", "leaf"),
        P(None, "leaf"),
        P("leaf", "rhs", None, None),
        P("leaf", "rhs"),
        P(),
        P("leaf", None),
        P("leaf", None, None, None),
        P("leaf", None, None, None),
        P(),
        P(),
    )
    out_specs = P("rhs", "leaf")
    return jax.shard_map(local, mesh=mesh, in_specs=in_specs, out_specs=out_specs, check_vma=False)
```

profile of v0, /device:TPU:192, one launch (start us, length us, event | category | flops | bytes accessed | tf_op | source)
XLA Modules:
  0.0 177.5 jit_solution(17345306287468822620)
XLA Ops:
  8.2 1.9 %collective-permute-start = (bf16[16,32,128]{2,0,1:T(8,128)(2,1)}, bf16[16,32,128]{2,0,1:T(8,128)(2,1)}, u32[]{:S(2)}, u32[]{:S(2)}) collective-permute-start(bf16[16,32,128]{2,0,1:T(8,128)(2,1)} %copy_bitcast_fusion.1), channel_id=1, source_target_pairs={{0,4},{4,8},{8,12},{12,16},{16,20},{20,24},{24,28},{28,32},{32,36}... | collective-permute-start | bytes 393224 | tf_op jit(solution)/shard_map/ppermute | solution.py:13
  10.1 5.8 %collective-permute-start.1 = (bf16[16,32,128]{2,0,1:T(8,128)(2,1)}, bf16[16,32,128]{2,0,1:T(8,128)(2,1)}, u32[]{:S(2)}, u32[]{:S(2)}) collective-permute-start(bf16[16,32,128]{2,0,1:T(8,128)(2,1)} %copy_bitcast_fusion.1), channel_id=1, source_target_pairs={{4,0},{8,4},{12,8},{16,12},{20,16},{24,20},{28,24},{32,28},{36,32}... | collective-permute-start | bytes 393224 | tf_op jit(solution)/shard_map/ppermute | solution.py:13
  15.9 3.0 %collective-permute-start.2 = (bf16[16,32,128]{2,0,1:T(8,128)(2,1)}, bf16[16,32,128]{2,0,1:T(8,128)(2,1)}, u32[]{:S(2)}, u32[]{:S(2)}) collective-permute-start(bf16[16,32,128]{2,0,1:T(8,128)(2,1)} %copy_bitcast_fusion.1), channel_id=1, source_target_pairs={{0,16},{4,20},{8,24},{12,28},{16,32},{20,36},{24,40},{28,44},{32,4... | collective-permute-start | bytes 393224 | tf_op jit(solution)/shard_map/ppermute | solution.py:13
  18.9 5.3 %collective-permute-start.3 = (bf16[16,32,128]{2,0,1:T(8,128)(2,1)}, bf16[16,32,128]{2,0,1:T(8,128)(2,1)}, u32[]{:S(2)}, u32[]{:S(2)}) collective-permute-start(bf16[16,32,128]{2,0,1:T(8,128)(2,1)} %copy_bitcast_fusion.1), channel_id=1, source_target_pairs={{16,0},{20,4},{24,8},{28,12},{32,16},{36,20},{40,24},{44,28},{48,3... | collective-permute-start | bytes 393224 | tf_op jit(solution)/shard_map/ppermute | solution.py:13
  33.1 10.9 %all-to-all-start = ((f32[64,1,512]{2,1,0:T(1,128)}), f32[64,1,512]{2,1,0:T(1,128)}, u32[]{:S(2)}, u32[]{:S(2)}) async-start(f32[64,1,512]{2,1,0:T(1,128)} %reshape.311), calls=%async_computation | async-start | bytes 262144 | tf_op jit(solution)/shard_map/all_to_all | solution.py:18
  52.7 10.2 %all-gather = s32[4,2,32]{2,1,0:T(2,128)S(1)} all-gather(s32[1,2,32]{2,1,0:T(2,128)S(1)} %bitcast.205), channel_id=1, replica_groups=mesh['leaf'=64,'rhs'=4] {'rhs'}, dimensions={0}, use_global_device_ids=true | all-gather | bytes 1280 | tf_op jit(solution)/shard_map/all_gather | solution.py:115
  63.7 2.4 %gather_fusion.1 = f32[256,16,32]{2,1,0:T(8,128)} fusion(f32[32,16,32]{2,1,0:T(8,128)S(1)} %fusion.24, s32[1024]{0:T(1024)S(1)} %pad_clamp_fusion), kind=kCustom, calls=%fused_computation.7 | custom fusion | bytes 1049600 | tf_op jit(solution)/shard_map/jit(_take)/gather | solution.py:137
  76.4 4.6 %fusion.2 = f32[32,16,32]{2,1,0:T(8,128)} fusion(f32[32,8,32,32]{3,2,1,0:T(8,128)S(1)} %copy-done.8, f32[32,8,16,32]{3,2,1,0:T(8,128)S(1)} %bitcast.192, pred[32,8]{1,0:T(8,128)(4,1)S(1)} %copy-done.35), kind=kOutput, calls=%fused_computation.10 | convolution fusion | flops 50462720 | bytes 1638656 | tf_op jit(solution)/shard_map/tjrs,tjqs->tqr/dot_general | solution.py:138
  86.6 2.4 %copy.161 = f32[32,1,32,32]{3,2,0,1:T(8,128)} copy(f32[32,1,32,32]{0,3,2,1:T(8,128)} %get-tuple-element.32) | data formatting | bytes 262144
  88.9 2.2 %copy.162 = f32[32,1,32,32]{3,2,0,1:T(8,128)} copy(f32[32,1,32,32]{0,3,2,1:T(8,128)} %get-tuple-element.31) | data formatting | bytes 262144
  92.4 2.0 %copy.171 = f32[8,1,32,32]{3,2,0,1:T(8,128)} copy(f32[8,1,32,32]{0,3,2,1:T(8,128)} %get-tuple-element.28) | data formatting | bytes 65536
  94.3 2.3 %copy.164 = f32[32,32,32]{2,1,0:T(8,128)} copy(f32[32,32,32]{0,2,1:T(8,128)} %slice.299) | data formatting | bytes 262144
  97.9 1.9 %copy.169 = f32[8,1,32,32]{3,2,0,1:T(8,128)} copy(f32[8,1,32,32]{0,3,2,1:T(8,128)} %get-tuple-element.29) | data formatting | bytes 65536
  99.8 1.9 %copy.170 = f32[8,1,32,32]{3,2,0,1:T(8,128)} copy(f32[8,1,32,32]{0,3,2,1:T(8,128)} %get-tuple-element.27) | data formatting | bytes 65536
  101.7 1.9 %copy.175 = f32[4,1,32,32]{3,2,0,1:T(8,128)} copy(f32[4,1,32,32]{0,3,2,1:T(8,128)} %get-tuple-element.26) | data formatting | bytes 32768
  103.9 2.0 %copy.173 = f32[4,1,32,32]{3,2,0,1:T(8,128)} copy(f32[4,1,32,32]{0,3,2,1:T(8,128)} %get-tuple-element.25) | data formatting | bytes 32768
  105.9 2.0 %copy.174 = f32[4,1,32,32]{3,2,0,1:T(8,128)} copy(f32[4,1,32,32]{0,3,2,1:T(8,128)} %get-tuple-element.24) | data formatting | bytes 32768
  107.8 2.0 %copy.167 = f32[16,1,32,32]{3,2,0,1:T(8,128)} copy(f32[16,1,32,32]{0,3,2,1:T(8,128)} %get-tuple-element.22) | data formatting | bytes 131072
  110.7 2.0 %copy.166 = f32[16,1,32,32]{3,2,0,1:T(8,128)} copy(f32[16,1,32,32]{0,3,2,1:T(8,128)} %get-tuple-element.21) | data formatting | bytes 131072
  112.8 2.9 %copy.159 = f32[64,1,32,32]{3,2,0,1:T(8,128)} copy(f32[64,1,32,32]{0,3,2,1:T(8,128)} %get-tuple-element.19) | data formatting | bytes 524288
  115.6 3.0 %copy.158 = f32[64,1,32,32]{3,2,0,1:T(8,128)} copy(f32[64,1,32,32]{0,3,2,1:T(8,128)} %get-tuple-element.20) | data formatting | bytes 524288
  121.4 4.2 %collective-permute-start.5 = (bf16[16,32,128]{2,0,1:T(8,128)(2,1)}, bf16[16,32,128]{2,0,1:T(8,128)(2,1)S(1)}, u32[]{:S(2)}, u32[]{:S(2)}) collective-permute-start(bf16[16,32,128]{2,0,1:T(8,128)(2,1)} %copy_bitcast_fusion.1), channel_id=1, source_target_pairs={{64,0},{68,4},{72,8},{76,12},{80,16},{84,20},{88,24},{92,28},{96,3... | collective-permute-start | bytes 393224 | tf_op jit(solution)/shard_map/ppermute | solution.py:13
  158.6 2.0 %fusion.12 = f32[64,16,32]{2,1,0:T(8,128)S(1)} fusion(f32[64,1,32,32]{3,2,0,1:T(8,128)S(1)} %copy-done.19, f32[64,1,16,32]{3,2,1,0:T(8,128)S(1)} %reshape.312), kind=kOutput, calls=%fused_computation.28 | convolution fusion | flops 12189696 | bytes 524288 | tf_op jit(solution)/shard_map/...nrs,...nqs->...nqr/dot_general | solution.py:47
  164.6 4.7 %convolution_bitcast_fusion = f32[32,16,128]{2,1,0:T(8,128)S(1)} fusion(bf16[32,8,128,128]{3,2,1,0:T(8,128)(2,1)} %all-gather.3.cloned.1.call-done, bf16[32,8,16,128]{3,2,1,0:T(8,128)(2,1)S(1)} %bitcast.194, pred[32,8]{1,0:T(8,128)(4,1)S(1)} %copy.111), kind=kOutput, calls=%fused_computation.17 | convolution fusion | flops 134742016 | bytes 9699584 | tf_op jit(solution)/shard_map/tkij,qtkj->qti/dot_general | solution.py:117
  (227 shorter events, 80.1 us)
Async XLA Ops:
  6.5 20.8 %copy-start = (f32[32,4096]{1,0:T(8,128)S(1)}, f32[32,4096]{1,0:T(8,128)}, u32[]{:S(2)}) copy-start(f32[32,4096]{1,0:T(8,128)} %param.13) | copy-start | bytes 1572868
  6.5 18.9 %copy-start.2 = (f32[1,64,32,32]{1,3,2,0:T(8,128)S(1)}, f32[1,64,32,32]{1,3,2,0:T(8,128)}, u32[]{:S(2)}) copy-start(f32[1,64,32,32]{1,3,2,0:T(8,128)} %param.19) | copy-start | bytes 786436
  6.5 158.1 %all-gather.3.cloned.1.call-start = ((), (), s32[]{:S(2)}) async-start(), calls=%async_computation.1 | async-start | bytes 10485760 | tf_op jit(solution)/shard_map/all_gather | solution.py:114
  8.2 113.2 %collective-permute-start = (bf16[16,32,128]{2,0,1:T(8,128)(2,1)}, bf16[16,32,128]{2,0,1:T(8,128)(2,1)}, u32[]{:S(2)}, u32[]{:S(2)}) collective-permute-start(bf16[16,32,128]{2,0,1:T(8,128)(2,1)} %copy_bitcast_fusion.1), channel_id=1, source_target_pairs={{0,4},{4,8},{8,12},{12,16},{16,20},{20,24},{24,28},{28,32},{32,36}... | collective-permute-start | bytes 393224 | tf_op jit(solution)/shard_map/ppermute | solution.py:13
  10.1 117.0 %collective-permute-start.1 = (bf16[16,32,128]{2,0,1:T(8,128)(2,1)}, bf16[16,32,128]{2,0,1:T(8,128)(2,1)}, u32[]{:S(2)}, u32[]{:S(2)}) collective-permute-start(bf16[16,32,128]{2,0,1:T(8,128)(2,1)} %copy_bitcast_fusion.1), channel_id=1, source_target_pairs={{4,0},{8,4},{12,8},{16,12},{20,16},{24,20},{28,24},{32,28},{36,32}... | collective-permute-start | bytes 393224 | tf_op jit(solution)/shard_map/ppermute | solution.py:13
  15.9 112.9 %collective-permute-start.2 = (bf16[16,32,128]{2,0,1:T(8,128)(2,1)}, bf16[16,32,128]{2,0,1:T(8,128)(2,1)}, u32[]{:S(2)}, u32[]{:S(2)}) collective-permute-start(bf16[16,32,128]{2,0,1:T(8,128)(2,1)} %copy_bitcast_fusion.1), channel_id=1, source_target_pairs={{0,16},{4,20},{8,24},{12,28},{16,32},{20,36},{24,40},{28,44},{32,4... | collective-permute-start | bytes 393224 | tf_op jit(solution)/shard_map/ppermute | solution.py:13
  18.9 111.5 %collective-permute-start.3 = (bf16[16,32,128]{2,0,1:T(8,128)(2,1)}, bf16[16,32,128]{2,0,1:T(8,128)(2,1)}, u32[]{:S(2)}, u32[]{:S(2)}) collective-permute-start(bf16[16,32,128]{2,0,1:T(8,128)(2,1)} %copy_bitcast_fusion.1), channel_id=1, source_target_pairs={{16,0},{20,4},{24,8},{28,12},{32,16},{36,20},{40,24},{44,28},{48,3... | collective-permute-start | bytes 393224 | tf_op jit(solution)/shard_map/ppermute | solution.py:13
  24.1 107.8 %collective-permute-start.4 = (bf16[16,32,128]{2,0,1:T(8,128)(2,1)}, bf16[16,32,128]{2,0,1:T(8,128)(2,1)}, u32[]{:S(2)}, u32[]{:S(2)}) collective-permute-start(bf16[16,32,128]{2,0,1:T(8,128)(2,1)} %copy_bitcast_fusion.1), channel_id=1, source_target_pairs={{0,64},{4,68},{8,72},{12,76},{16,80},{20,84},{24,88},{28,92},{32,9... | collective-permute-start | bytes 393224 | tf_op jit(solution)/shard_map/ppermute | solution.py:13
  30.1 13.9 %copy-start.33 = (s32[64,6,4]{0,2,1:T(4,128)S(1)}, s32[64,6,4]{0,2,1:T(4,128)}, u32[]{:S(2)}) copy-start(s32[64,6,4]{0,2,1:T(4,128)} %param.16) | copy-start | bytes 18436
  30.1 22.7 %copy-start.37 = (s32[32,2]{0,1:T(2,128)S(1)}, s32[32,2]{0,1:T(2,128)}, u32[]{:S(2)}) copy-start(s32[32,2]{0,1:T(2,128)} %param.15) | copy-start | bytes 772
  30.6 32.4 %copy-start.34 = (s32[32,8]{0,1:T(8,128)S(1)}, s32[32,8]{0,1:T(8,128)}, u32[]{:S(2)}) copy-start(s32[32,8]{0,1:T(8,128)} %param.17) | copy-start | bytes 3076
  33.1 107.3 %all-to-all-start = ((f32[64,1,512]{2,1,0:T(1,128)}), f32[64,1,512]{2,1,0:T(1,128)}, u32[]{:S(2)}, u32[]{:S(2)}) async-start(f32[64,1,512]{2,1,0:T(1,128)} %reshape.311), calls=%async_computation | async-start | bytes 262144 | tf_op jit(solution)/shard_map/all_to_all | solution.py:18
  70.6 4.8 %copy-start.35 = (pred[32,8]{1,0:T(8,128)(4,1)S(1)}, pred[32,8]{1,0:T(8,128)(4,1)}, u32[]{:S(2)}) copy-start(pred[32,8]{1,0:T(8,128)(4,1)} %copy.146) | copy-start | bytes 772
  76.4 5.1 %copy-start.3 = (f32[128,32,32]{0,2,1:T(8,128)S(1)}, f32[128,32,32]{0,2,1:T(8,128)}, u32[]{:S(2)}) copy-start(f32[128,32,32]{0,2,1:T(8,128)} %param.20) | copy-start | bytes 1572868
  81.5 4.0 %copy-start.36 = (pred[32,8]{0,1:T(8,128)(4,1)S(1)}, pred[32,8]{0,1:T(8,128)(4,1)}, u32[]{:S(2)}) copy-start(pred[32,8]{0,1:T(8,128)(4,1)} %compare_and_fusion.1) | copy-start | bytes 772
  86.6 4.6 %copy-start.13 = (f32[32,1,32,32]{0,3,2,1:T(8,128)S(1)}, f32[32,1,32,32]{0,3,2,1:T(8,128)}, u32[]{:S(2)}) copy-start(f32[32,1,32,32]{0,3,2,1:T(8,128)} %get-tuple-element.30) | copy-start | bytes 393220
  92.4 11.3 %copy-start.10 = (f32[8,32,32]{0,2,1:T(8,128)S(1)}, f32[8,32,32]{0,2,1:T(8,128)}, u32[]{:S(2)}) copy-start(f32[8,32,32]{0,2,1:T(8,128)} %slice.319) | copy-start | bytes 98308
  103.9 5.9 %copy-start.12 = (f32[16,1,32,32]{0,3,2,1:T(8,128)S(1)}, f32[16,1,32,32]{0,3,2,1:T(8,128)}, u32[]{:S(2)}) copy-start(f32[16,1,32,32]{0,3,2,1:T(8,128)} %get-tuple-element.23) | copy-start | bytes 196612
  110.7 8.0 %copy-start.11 = (f32[64,1,32,32]{0,3,2,1:T(8,128)S(1)}, f32[64,1,32,32]{0,3,2,1:T(8,128)}, u32[]{:S(2)}) copy-start(f32[64,1,32,32]{0,3,2,1:T(8,128)} %get-tuple-element.18) | copy-start | bytes 786436
  121.4 15.7 %collective-permute-start.5 = (bf16[16,32,128]{2,0,1:T(8,128)(2,1)}, bf16[16,32,128]{2,0,1:T(8,128)(2,1)S(1)}, u32[]{:S(2)}, u32[]{:S(2)}) collective-permute-start(bf16[16,32,128]{2,0,1:T(8,128)(2,1)} %copy_bitcast_fusion.1), channel_id=1, source_target_pairs={{64,0},{68,4},{72,8},{76,12},{80,16},{84,20},{88,24},{92,28},{96,3... | collective-permute-start | bytes 393224 | tf_op jit(solution)/shard_map/ppermute | solution.py:13
  144.0 4.0 %copy-start.23 = (f32[8,1,32,32]{3,2,0,1:T(8,128)S(1)}, f32[8,1,32,32]{3,2,0,1:T(8,128)}, u32[]{:S(2)}) copy-start(f32[8,1,32,32]{3,2,0,1:T(8,128)} %copy.170) | copy-start | bytes 98308
  144.1 4.6 %copy-start.18 = (f32[16,1,32,32]{3,2,0,1:T(8,128)S(1)}, f32[16,1,32,32]{3,2,0,1:T(8,128)}, u32[]{:S(2)}) copy-start(f32[16,1,32,32]{3,2,0,1:T(8,128)} %copy.167) | copy-start | bytes 196612
  144.1 4.6 %copy-start.40 = (pred[16]{0:T(512)(128)(4,1)S(1)}, pred[16]{0:T(512)(128)(4,1)}, u32[]{:S(2)}) copy-start(pred[16]{0:T(512)(128)(4,1)} %fusion.103) | copy-start | bytes 52
  145.9 3.9 %copy-start.28 = (f32[16,1,32,32]{3,2,0,1:T(8,128)S(1)}, f32[16,1,32,32]{3,2,0,1:T(8,128)}, u32[]{:S(2)}) copy-start(f32[16,1,32,32]{3,2,0,1:T(8,128)} %copy.165) | copy-start | bytes 196612
  (27 other events, 67.4 us)
Sparse Core Ops, SparseCore 0:
  25.6 87.3 all-gather.2
where the time goes:
time: 179 us; the launch traced here: 178 us
  local copies, waits for them, and re-layouts  70.7 us (39%)
  matrix products  32.5 us (18%)
  starting transfers between devices  32.2 us (18%)
  other arithmetic  17.6 us (10%)
  between operations  14.3 us (8%)
  blocking collectives  10.2 us (6%)
    unnamed x113, local copies, waits for them, and re-layouts  39.9 us
    ppermute x6, starting transfers between devices, shifted(): lax.ppermute(value, axis, [(source, source + steps) for source in range(f...  21.4 us
    dot_general x24, matrix products, apply_maps(): jnp.einsum('...nrs,...nqs->...nqr', node_maps, coef_rows, precision=TOP_P...  17.2 us
    all_to_all x1, starting transfers between devices, from_everyone(): return lax.all_to_all(copies, axis, split_axis=0, concat_axis=0, tiled=True)  10.9 us
    all_gather x1, blocking collectives, local(): piece_sources = lax.all_gather(near_src, 'rhs', axis=1, tiled=True)  10.2 us
    gather x6, local copies, waits for them, and re-layouts, local(): chosen = jnp.take(neighbour_panels, jnp.maximum(sent_leaf, 0), axis=1)  8.61 us
    dot_general x9, matrix products, lift_pairs(): jnp.einsum('...nrs,...nqr->...nqs', child_maps, child_coef, precision=TOP...  4.9 us
    slice x3, local copies, waits for them, and re-layouts, couple_level(): maps_level[:, 1]  4.84 us
  transfers between devices with their start and end apart: 8, of which 0 were waited for; matrix products, arithmetic and copies ran while one was open for 63% of the time, Pallas kernels for 0%

commit v1 on v0

--- a/solution.py
+++ b/solution.py
@@ -112,7 +112,10 @@
         arrived.append(jnp.where(keep_slot[None, :, None], chosen, jnp.zeros_like(chosen)))
     buffer = jnp.concatenate([panels] + arrived, axis=1)
     piece_blocks = lax.all_gather(near_blocks, "rhs", axis=1, tiled=True)
-    piece_sources = lax.all_gather(near_src, "rhs", axis=1, tiled=True)
+    devices = lax.axis_size("rhs")
+    pieces = jnp.stack([near_src for _ in range(devices)])
+    pieces = lax.all_to_all(pieces, "rhs", split_axis=0, concat_axis=0)
+    piece_sources = jnp.concatenate(pieces, axis=1)
     picked = jnp.take(buffer, piece_sources, axis=1)
     near_field = jnp.einsum(
         "tkij,qtkj->qti", piece_blocks, picked, preferred_element_type=jnp.float32

time: 179 us -> 183 us (1.022)
  the two profiles are of different devices: /device:TPU:192 before, /device:TPU:10 now
where the time goes in v1:
time: 183 us; the launch traced here: 181 us
  local copies, waits for them, and re-layouts  78.3 us (43%)
  starting transfers between devices  36.4 us (20%)
  matrix products  34.1 us (19%)
  other arithmetic  15.6 us (9%)
  between operations  14.5 us (8%)
  waiting for transfers between devices  2.32 us (1%)
    unnamed x137, local copies, waits for them, and re-layouts  44.4 us
    ppermute x6, starting transfers between devices, shifted(): lax.ppermute(value, axis, [(source, source + steps) for source in range(f...  20.9 us
    dot_general x24, matrix products, apply_maps(): jnp.einsum('...nrs,...nqs->...nqr', node_maps, coef_rows, precision=TOP_P...  17.2 us
    all_to_all x1, starting transfers between devices, from_everyone(): return lax.all_to_all(copies, axis, split_axis=0, concat_axis=0, tiled=True)  10.6 us
    gather x6, local copies, waits for them, and re-layouts, local(): chosen = jnp.take(neighbour_panels, jnp.maximum(sent_leaf, 0), axis=1)  8.61 us
    dot_general x1, matrix products, local(): jnp.einsum('tjrs,tjqs->tqr', leaf_coupling, picked_coef, precision=TOP_PREC)  7.38 us
    and x6, other arithmetic, local(): chosen = jnp.take(neighbour_panels, jnp.maximum(sent_leaf, 0), axis=1)  7.17 us
    slice x5, local copies, waits for them, and re-layouts, local(): subtree_maps[level_width:2 * level_width]  5.01 us
  transfers between devices with their start and end apart: 9, of which 1 were waited for; matrix products, arithmetic and copies ran while one was open for 66% of the time, Pallas kernels for 0%

profile of v1, /device:TPU:10, one launch (start us, length us, event | category | flops | bytes accessed | tf_op | source)
XLA Modules:
  0.0 181.2 jit_solution(10710418139337456034)
XLA Ops:
  8.2 1.9 %collective-permute-start = (bf16[16,32,128]{2,0,1:T(8,128)(2,1)}, bf16[16,32,128]{2,0,1:T(8,128)(2,1)}, u32[]{:S(2)}, u32[]{:S(2)}) collective-permute-start(bf16[16,32,128]{2,0,1:T(8,128)(2,1)} %copy_bitcast_fusion.1), channel_id=1, source_target_pairs={{0,4},{4,8},{8,12},{12,16},{16,20},{20,24},{24,28},{28,32},{32,36}... | collective-permute-start | bytes 393224 | tf_op jit(solution)/shard_map/ppermute | solution.py:13
  10.1 3.6 %collective-permute-start.1 = (bf16[16,32,128]{2,0,1:T(8,128)(2,1)}, bf16[16,32,128]{2,0,1:T(8,128)(2,1)}, u32[]{:S(2)}, u32[]{:S(2)}) collective-permute-start(bf16[16,32,128]{2,0,1:T(8,128)(2,1)} %copy_bitcast_fusion.1), channel_id=1, source_target_pairs={{4,0},{8,4},{12,8},{16,12},{20,16},{24,20},{28,24},{32,28},{36,32}... | collective-permute-start | bytes 393224 | tf_op jit(solution)/shard_map/ppermute | solution.py:13
  13.8 4.9 %collective-permute-start.2 = (bf16[16,32,128]{2,0,1:T(8,128)(2,1)}, bf16[16,32,128]{2,0,1:T(8,128)(2,1)}, u32[]{:S(2)}, u32[]{:S(2)}) collective-permute-start(bf16[16,32,128]{2,0,1:T(8,128)(2,1)} %copy_bitcast_fusion.1), channel_id=1, source_target_pairs={{0,16},{4,20},{8,24},{12,28},{16,32},{20,36},{24,40},{28,44},{32,4... | collective-permute-start | bytes 393224 | tf_op jit(solution)/shard_map/ppermute | solution.py:13
  19.9 8.0 %collective-permute-start.4 = (bf16[16,32,128]{2,0,1:T(8,128)(2,1)}, bf16[16,32,128]{2,0,1:T(8,128)(2,1)}, u32[]{:S(2)}, u32[]{:S(2)}) collective-permute-start(bf16[16,32,128]{2,0,1:T(8,128)(2,1)} %copy_bitcast_fusion.1), channel_id=1, source_target_pairs={{0,64},{4,68},{8,72},{12,76},{16,80},{20,84},{24,88},{28,92},{32,9... | collective-permute-start | bytes 393224 | tf_op jit(solution)/shard_map/ppermute | solution.py:13
  28.5 4.8 %all-to-all-start = ((s32[4,32,2]{1,2,0:T(2,128)}), s32[4,32,2]{1,2,0:T(2,128)S(1)}, u32[]{:S(2)}, u32[]{:S(2)}) async-start(s32[4,32,2]{1,2,0:T(2,128)} %stack.2), calls=%async_computation | async-start | bytes 8192 | tf_op jit(solution)/shard_map/all_to_all | solution.py:117
  57.8 1.9 %copy.156 = f32[1,2,32,32]{3,2,1,0:T(8,128)} copy(f32[1,2,32,32]{1,3,2,0:T(8,128)} %slice.278) | data formatting | bytes 16384
  60.7 2.0 %copy.155 = f32[1,4,32,32]{3,2,1,0:T(8,128)} copy(f32[1,4,32,32]{1,3,2,0:T(8,128)} %slice.274) | data formatting | bytes 32768
  66.4 2.4 %gather_fusion.1 = f32[256,16,32]{2,1,0:T(8,128)} fusion(f32[32,16,32]{2,1,0:T(8,128)S(1)} %fusion.24, s32[1024]{0:T(1024)S(1)} %pad_clamp_fusion), kind=kCustom, calls=%fused_computation.7 | custom fusion | bytes 1049600 | tf_op jit(solution)/shard_map/jit(_take)/gather | solution.py:140
  71.3 2.2 %copy.161 = f32[32,1,32,32]{3,2,0,1:T(8,128)} copy(f32[32,1,32,32]{0,3,2,1:T(8,128)} %get-tuple-element.32) | data formatting | bytes 262144
  73.6 2.3 %copy.162 = f32[32,1,32,32]{3,2,0,1:T(8,128)} copy(f32[32,1,32,32]{0,3,2,1:T(8,128)} %get-tuple-element.31) | data formatting | bytes 262144
  77.1 2.0 %copy.171 = f32[8,1,32,32]{3,2,0,1:T(8,128)} copy(f32[8,1,32,32]{0,3,2,1:T(8,128)} %get-tuple-element.28) | data formatting | bytes 65536
  80.5 2.0 %copy.168 = f32[16,32,32]{2,1,0:T(8,128)} copy(f32[16,32,32]{0,2,1:T(8,128)} %slice.309) | data formatting | bytes 131072
  86.3 2.0 %copy.175 = f32[4,1,32,32]{3,2,0,1:T(8,128)} copy(f32[4,1,32,32]{0,3,2,1:T(8,128)} %get-tuple-element.26) | data formatting | bytes 32768
  89.1 2.0 %copy.173 = f32[4,1,32,32]{3,2,0,1:T(8,128)} copy(f32[4,1,32,32]{0,3,2,1:T(8,128)} %get-tuple-element.25) | data formatting | bytes 32768
  91.1 2.0 %copy.174 = f32[4,1,32,32]{3,2,0,1:T(8,128)} copy(f32[4,1,32,32]{0,3,2,1:T(8,128)} %get-tuple-element.24) | data formatting | bytes 32768
  93.1 2.0 %copy.167 = f32[16,1,32,32]{3,2,0,1:T(8,128)} copy(f32[16,1,32,32]{0,3,2,1:T(8,128)} %get-tuple-element.22) | data formatting | bytes 131072
  96.0 2.0 %copy.166 = f32[16,1,32,32]{3,2,0,1:T(8,128)} copy(f32[16,1,32,32]{0,3,2,1:T(8,128)} %get-tuple-element.21) | data formatting | bytes 131072
  98.1 2.8 %copy.159 = f32[64,1,32,32]{3,2,0,1:T(8,128)} copy(f32[64,1,32,32]{0,3,2,1:T(8,128)} %get-tuple-element.19) | data formatting | bytes 524288
  100.9 3.0 %copy.158 = f32[64,1,32,32]{3,2,0,1:T(8,128)} copy(f32[64,1,32,32]{0,3,2,1:T(8,128)} %get-tuple-element.20) | data formatting | bytes 524288
  112.9 7.4 %fusion.2 = f32[32,16,32]{2,1,0:T(8,128)} fusion(f32[32,8,32,32]{3,2,1,0:T(8,128)} %param.18, f32[32,8,16,32]{3,2,1,0:T(8,128)} %bitcast.193, pred[32,8]{1,0:T(8,128)(4,1)} %copy.146), kind=kOutput, calls=%fused_computation.10 | convolution fusion | flops 50462720 | bytes 1638656 | tf_op jit(solution)/shard_map/tjrs,tjqs->tqr/dot_general | solution.py:141
  120.6 10.6 %all-to-all-start.1 = ((f32[64,1,512]{2,1,0:T(1,128)}), f32[64,1,512]{2,1,0:T(1,128)S(1)}, u32[]{:S(2)}, u32[]{:S(2)}) async-start(f32[64,1,512]{2,1,0:T(1,128)} %reshape.350), calls=%async_computation.1 | async-start | bytes 262144 | tf_op jit(solution)/shard_map/all_to_all | solution.py:18
  141.3 2.3 %collective-permute-done.5 = bf16[16,32,128]{2,0,1:T(8,128)(2,1)S(1)} collective-permute-done((bf16[16,32,128]{2,0,1:T(8,128)(2,1)}, bf16[16,32,128]{2,0,1:T(8,128)(2,1)S(1)}, u32[]{:S(2)}, u32[]{:S(2)}) %collective-permute-start.5) | collective-permute-done | bytes 131104 | tf_op jit(solution)/shard_map/ppermute | solution.py:13
  162.3 1.9 %fusion.12 = f32[64,16,32]{2,1,0:T(8,128)S(1)} fusion(f32[64,1,32,32]{3,2,0,1:T(8,128)S(1)} %copy-done.19, f32[64,1,16,32]{3,2,1,0:T(8,128)S(1)} %reshape.351), kind=kOutput, calls=%fused_computation.28 | convolution fusion | flops 12189696 | bytes 524288 | tf_op jit(solution)/shard_map/...nrs,...nqs->...nqr/dot_general | solution.py:47
  168.3 4.7 %convolution_bitcast_fusion = f32[32,16,128]{2,1,0:T(8,128)S(1)} fusion(bf16[32,8,128,128]{3,2,1,0:T(8,128)(2,1)} %all-gather.2.cloned.1.call-done, bf16[32,8,16,128]{3,2,1,0:T(8,128)(2,1)S(1)} %bitcast.195, pred[32,8]{1,0:T(8,128)(4,1)S(1)} %copy.111), kind=kOutput, calls=%fused_computation.17 | convolution fusion | flops 134742016 | bytes 9699584 | tf_op jit(solution)/shard_map/tkij,qtkj->qti/dot_general | solution.py:120
  (254 shorter events, 86.1 us)
Async XLA Ops:
  6.5 49.9 %copy-start = (f32[32,4096]{1,0:T(8,128)S(1)}, f32[32,4096]{1,0:T(8,128)}, u32[]{:S(2)}) copy-start(f32[32,4096]{1,0:T(8,128)} %param.13) | copy-start | bytes 1572868
  6.5 21.4 %copy-start.37 = (s32[32,2]{0,1:T(2,128)S(1)}, s32[32,2]{0,1:T(2,128)}, u32[]{:S(2)}) copy-start(s32[32,2]{0,1:T(2,128)} %param.15) | copy-start | bytes 772
  6.5 26.8 %copy-start.36 = (s32[32,8]{0,1:T(8,128)S(1)}, s32[32,8]{0,1:T(8,128)}, u32[]{:S(2)}) copy-start(s32[32,8]{0,1:T(8,128)} %param.17) | copy-start | bytes 3076
  6.5 26.8 %copy-start.2 = (f32[1,64,32,32]{1,3,2,0:T(8,128)S(1)}, f32[1,64,32,32]{1,3,2,0:T(8,128)}, u32[]{:S(2)}) copy-start(f32[1,64,32,32]{1,3,2,0:T(8,128)} %param.19) | copy-start | bytes 786436
  6.5 161.7 %all-gather.2.cloned.1.call-start = ((), (), s32[]{:S(2)}) async-start(), calls=%async_computation.2 | async-start | bytes 10485760 | tf_op jit(solution)/shard_map/all_gather | solution.py:114
  8.2 123.3 %collective-permute-start = (bf16[16,32,128]{2,0,1:T(8,128)(2,1)}, bf16[16,32,128]{2,0,1:T(8,128)(2,1)}, u32[]{:S(2)}, u32[]{:S(2)}) collective-permute-start(bf16[16,32,128]{2,0,1:T(8,128)(2,1)} %copy_bitcast_fusion.1), channel_id=1, source_target_pairs={{0,4},{4,8},{8,12},{12,16},{16,20},{20,24},{24,28},{28,32},{32,36}... | collective-permute-start | bytes 393224 | tf_op jit(solution)/shard_map/ppermute | solution.py:13
  10.1 124.3 %collective-permute-start.1 = (bf16[16,32,128]{2,0,1:T(8,128)(2,1)}, bf16[16,32,128]{2,0,1:T(8,128)(2,1)}, u32[]{:S(2)}, u32[]{:S(2)}) collective-permute-start(bf16[16,32,128]{2,0,1:T(8,128)(2,1)} %copy_bitcast_fusion.1), channel_id=1, source_target_pairs={{4,0},{8,4},{12,8},{16,12},{20,16},{24,20},{28,24},{32,28},{36,32}... | collective-permute-start | bytes 393224 | tf_op jit(solution)/shard_map/ppermute | solution.py:13
  13.8 122.2 %collective-permute-start.2 = (bf16[16,32,128]{2,0,1:T(8,128)(2,1)}, bf16[16,32,128]{2,0,1:T(8,128)(2,1)}, u32[]{:S(2)}, u32[]{:S(2)}) collective-permute-start(bf16[16,32,128]{2,0,1:T(8,128)(2,1)} %copy_bitcast_fusion.1), channel_id=1, source_target_pairs={{0,16},{4,20},{8,24},{12,28},{16,32},{20,36},{24,40},{28,44},{32,4... | collective-permute-start | bytes 393224 | tf_op jit(solution)/shard_map/ppermute | solution.py:13
  18.7 118.9 %collective-permute-start.3 = (bf16[16,32,128]{2,0,1:T(8,128)(2,1)}, bf16[16,32,128]{2,0,1:T(8,128)(2,1)}, u32[]{:S(2)}, u32[]{:S(2)}) collective-permute-start(bf16[16,32,128]{2,0,1:T(8,128)(2,1)} %copy_bitcast_fusion.1), channel_id=1, source_target_pairs={{16,0},{20,4},{24,8},{28,12},{32,16},{36,20},{40,24},{44,28},{48,3... | collective-permute-start | bytes 393224 | tf_op jit(solution)/shard_map/ppermute | solution.py:13
  19.9 119.2 %collective-permute-start.4 = (bf16[16,32,128]{2,0,1:T(8,128)(2,1)}, bf16[16,32,128]{2,0,1:T(8,128)(2,1)}, u32[]{:S(2)}, u32[]{:S(2)}) collective-permute-start(bf16[16,32,128]{2,0,1:T(8,128)(2,1)} %copy_bitcast_fusion.1), channel_id=1, source_target_pairs={{0,64},{4,68},{8,72},{12,76},{16,80},{20,84},{24,88},{28,92},{32,9... | collective-permute-start | bytes 393224 | tf_op jit(solution)/shard_map/ppermute | solution.py:13
  28.5 92.0 %all-to-all-start = ((s32[4,32,2]{1,2,0:T(2,128)}), s32[4,32,2]{1,2,0:T(2,128)S(1)}, u32[]{:S(2)}, u32[]{:S(2)}) async-start(s32[4,32,2]{1,2,0:T(2,128)} %stack.2), calls=%async_computation | async-start | bytes 8192 | tf_op jit(solution)/shard_map/all_to_all | solution.py:117
  51.9 10.8 %copy-start.9 = (f32[1,8,32,32]{1,3,2,0:T(8,128)S(1)}, f32[1,8,32,32]{1,3,2,0:T(8,128)}, u32[]{:S(2)}) copy-start(f32[1,8,32,32]{1,3,2,0:T(8,128)} %slice.270) | copy-start | bytes 98308
  52.7 10.8 %copy-start.49 = (s32[4]{0:T(128)}, s32[4]{0:T(128)S(1)}, u32[]{:S(2)}) copy-start(s32[4]{0:T(128)S(1)} %get-tuple-element.12) | copy-start | bytes 52
  52.8 10.8 %copy-start.50 = (s32[4]{0:T(128)}, s32[4]{0:T(128)S(1)}, u32[]{:S(2)}) copy-start(s32[4]{0:T(128)S(1)} %get-tuple-element.13) | copy-start | bytes 52
  52.8 10.7 %copy-start.51 = (s32[4]{0:T(128)}, s32[4]{0:T(128)S(1)}, u32[]{:S(2)}) copy-start(s32[4]{0:T(128)S(1)} %get-tuple-element.14) | copy-start | bytes 52
  77.1 11.2 %copy-start.8 = (f32[8,32,32]{0,2,1:T(8,128)S(1)}, f32[8,32,32]{0,2,1:T(8,128)}, u32[]{:S(2)}) copy-start(f32[8,32,32]{0,2,1:T(8,128)} %slice.319) | copy-start | bytes 98308
  112.8 28.0 %copy-start.48 = (pred[4]{0:T(512)(128)(4,1)S(1)}, pred[4]{0:T(512)(128)(4,1)}, u32[]{:S(2)}) copy-start(pred[4]{0:T(512)(128)(4,1)} %compare_and_fusion.7) | copy-start | bytes 16
  112.8 28.0 %copy-start.47 = (pred[4]{0:T(512)(128)(4,1)S(1)}, pred[4]{0:T(512)(128)(4,1)}, u32[]{:S(2)}) copy-start(pred[4]{0:T(512)(128)(4,1)} %compare_and_fusion.6) | copy-start | bytes 16
  112.9 28.1 %copy-start.46 = (pred[4]{0:T(512)(128)(4,1)S(1)}, pred[4]{0:T(512)(128)(4,1)}, u32[]{:S(2)}) copy-start(pred[4]{0:T(512)(128)(4,1)} %compare_and_fusion.5) | copy-start | bytes 16
  112.9 28.2 %copy-start.45 = (pred[4]{0:T(512)(128)(4,1)S(1)}, pred[4]{0:T(512)(128)(4,1)}, u32[]{:S(2)}) copy-start(pred[4]{0:T(512)(128)(4,1)} %compare_and_fusion.4) | copy-start | bytes 16
  112.9 28.3 %copy-start.44 = (pred[4]{0:T(512)(128)(4,1)S(1)}, pred[4]{0:T(512)(128)(4,1)}, u32[]{:S(2)}) copy-start(pred[4]{0:T(512)(128)(4,1)} %compare_and_fusion.3) | copy-start | bytes 16
  112.9 31.3 %copy-start.43 = (pred[4]{0:T(512)(128)(4,1)S(1)}, pred[4]{0:T(512)(128)(4,1)}, u32[]{:S(2)}) copy-start(pred[4]{0:T(512)(128)(4,1)} %compare_and_fusion.2) | copy-start | bytes 16
  120.6 25.6 %all-to-all-start.1 = ((f32[64,1,512]{2,1,0:T(1,128)}), f32[64,1,512]{2,1,0:T(1,128)S(1)}, u32[]{:S(2)}, u32[]{:S(2)}) async-start(f32[64,1,512]{2,1,0:T(1,128)} %reshape.350), calls=%async_computation.1 | async-start | bytes 262144 | tf_op jit(solution)/shard_map/all_to_all | solution.py:18
  131.5 12.0 %collective-permute-start.5 = (bf16[16,32,128]{2,0,1:T(8,128)(2,1)}, bf16[16,32,128]{2,0,1:T(8,128)(2,1)S(1)}, u32[]{:S(2)}, u32[]{:S(2)}) collective-permute-start(bf16[16,32,128]{2,0,1:T(8,128)(2,1)} %copy_bitcast_fusion.1), channel_id=1, source_target_pairs={{64,0},{68,4},{72,8},{76,12},{80,16},{84,20},{88,24},{92,28},{96,3... | collective-permute-start | bytes 393224 | tf_op jit(solution)/shard_map/ppermute | solution.py:13
  (40 other events, 140.4 us)
Sparse Core Ops, SparseCore 0:
  28.0 86.9 all-gather.1
